TPU v7x, 512 devices: a whole 4x8x8 slice. The times are simulated.
512 devices in a mesh: rows: 64 (over x, y, z_lo), cols: 8 (over z_hi, core).
Axes of the slice: x: 4, y: 8, z: 8 (z_hi: 4, z_lo: 2; z = z_hi * 2 + z_lo), core: 2. Of those that a mesh axis runs over, the one named last changes fastest.
Arguments:
- design: float32 [65536, 4096], P('rows', 'cols')
- signs: int32 [65536], P('rows'), may hold values from -1 to 1, as said below
- response: float32 [65536], P('rows'), may hold values from -6 to 6
- picks: int32 [8192], replicated, may hold values from 0 to 65535, as said below
Outputs:
- gram_blocks: float32 [512, 8, 512], P('rows', 'cols')
- rhs: float32 [4096], P('cols')
Inputs may be any that keep to these rules, and one draw needn't show every extreme that they name: `signs`: every entry is +1 or -1. `picks`: strictly increasing, all distinct; the first and the last row are always sampled.
All inputs are finite; a program needn't handle non-finite values.
Results may differ from a plain program's by a relative error of at most 0.0003.
Values sent between devices are 32-bit elements; how exact they have to be, the bound alone decides.
A program may use at most 64 MiB of HBM per device.

v0:
```python
import jax
import jax.numpy as jnp
from jax import lax
from jax.sharding import PartitionSpec as P

D = 4096
BW = 512
epsilon = 1e-06


def sylvester(order, dtype):
    row_ids = lax.broadcasted_iota(jnp.int32, (order, order), 0)
    col_ids = lax.broadcasted_iota(jnp.int32, (order, order), 1)
    common = jnp.bitwise_and(row_ids, col_ids)
    return (1 - 2 * jnp.bitwise_and(lax.population_count(common), 1)).astype(dtype)


def halves(values):
    top = lax.reduce_precision(values, 8, 7)
    rest = values - top
    return (top.astype(jnp.bfloat16), rest.astype(jnp.bfloat16))


def thirds(values):
    top = lax.reduce_precision(values, 8, 7)
    rest = values - top
    mid = lax.reduce_precision(rest, 8, 7)
    low = rest - mid
    return tuple((part.astype(jnp.bfloat16) for part in (top, mid, low)))


def dot(left, right):
    return jnp.dot(left, right, preferred_element_type=jnp.float32)


def mix(order, values):
    matrix = sylvester(order, jnp.bfloat16)
    return sum((dot(matrix, part) for part in halves(values)))


def local(design, signs, response, picks):
    height, width = design.shape
    groups = lax.axis_size("rows")
    position = lax.axis_index("rows")
    share = height // groups
    flips = signs.astype(jnp.float32)
    whole = lax.all_gather(response * flips, "rows", axis=0, tiled=True)
    side = 256
    square = whole.reshape(side, side)
    h_side = sylvester(side, jnp.bfloat16)
    square = sum((dot(h_side, part) for part in thirds(square)))
    square = sum((dot(part, h_side) for part in thirds(square)))
    answer = square.reshape(groups, groups, share)
    answer = lax.dynamic_slice_in_dim(answer, position, 1, axis=1)[:, 0, :]
    mixed = mix(height, design * flips[:, None])
    mixed = lax.all_to_all(
        mixed.reshape(groups, share, width), "rows", split_axis=0, concat_axis=0, tiled=True
    )
    mixed = mix(groups, mixed.reshape(groups, share * width)).reshape(height, width)
    group_of = picks // height
    inside = picks % height - position * share
    of_group = (lax.iota(jnp.int32, groups)[:, None] == group_of[None, :]).astype(jnp.bfloat16)
    of_local = (inside[:, None] == lax.iota(jnp.int32, share)[None, :]).astype(jnp.bfloat16)
    picked = dot(of_group, of_local)
    picked_answer = picked * answer
    chosen = mixed * picked.reshape(height)[:, None]
    top, rest = halves(chosen)

    def outer(left, right):
        return lax.dot_general(
            left, right, (((0,), (0,)), ((), ())), preferred_element_type=jnp.float32
        )

    cross = outer(top, rest)
    gram = outer(top, top) + cross + cross.T
    rhs_part = jnp.sum(chosen * picked_answer.reshape(height)[:, None], axis=0)
    power_part = jnp.sum(picked_answer * picked_answer)
    trace_part = jnp.sum(chosen * chosen)
    trace_sum = lax.psum(trace_part, ("rows", "cols"))
    blocks = gram.reshape(groups, BW // groups, width)
    extra = jnp.stack([rhs_part, jnp.full((width,), power_part)])
    extra = jnp.broadcast_to(extra[None], (groups, 2, width))
    parts = jnp.concatenate([blocks, extra], axis=1)
    parts = lax.all_to_all(parts, "rows", split_axis=0, concat_axis=0, tiled=True)
    sums = jnp.sum(parts, axis=0)
    mean_diag = trace_sum / D + epsilon
    gram_blocks = sums[: BW // groups, None, :] / mean_diag
    samples = picks.shape[0]
    rhs = (
        sums[BW // groups]
        * jnp.sqrt(jnp.float32(samples))
        / jnp.sqrt(mean_diag * sums[BW // groups + 1])
    )
    return (gram_blocks, rhs)


def solution(mesh):
    in_specs = (P("rows", "cols"), P("rows"), P("rows"), P())
    out_specs = (P("rows", "cols", None), P("cols"))
    return jax.shard_map(local, mesh=mesh, in_specs=in_specs, out_specs=out_specs, check_vma=False)
```

profile of v0, /device:TPU:27, one launch (start us, length us, event | category | flops | bytes accessed | tf_op | source)
XLA Modules:
  0.0 366.3 jit_solution(7511353022532499297)
XLA Ops:
  0.6 0.7 convert_element_type.74
  1.3 3.2 fusion.3
  4.5 2.7 fusion.6
  7.2 11.7 %all-to-all-start = ((f32[64,16,512]{2,1,0:T(8,128)}), f32[64,16,512]{2,1,0:T(8,128)S(1)}, u32[]{:S(2)}, u32[]{:S(2)}) async-start(f32[64,16,512]{2,1,0:T(8,128)} %bitcast.23), calls=%async_computation | async-start | bytes 4194304 | tf_op jit(solution)/shard_map/all_to_all | solution.py:56
  19.0 136.0 %all_gather.3 = f32[65536]{0:T(1024)S(1)} all-gather(f32[1024]{0:T(1024)S(1)} %convert_multiply_fusion), channel_id=1, replica_groups=mesh['rows'=64,'cols'=8] {'rows'}, dimensions={0}, use_global_device_ids=true | all-gather | bytes 266240 | tf_op jit(solution)/shard_map/all_gather | solution.py:47
  155.3 0.2 convolution_add_fusion.5
  155.5 0.2 convolution_add_fusion.4
  155.7 0.2 fusion.21
  155.9 0.2 convolution_add_fusion.3
  156.2 0.2 convolution_add_fusion.2
  156.4 2.0 reshape.59
  158.4 1.0 constant_dynamic-slice_fusion
  159.4 1.1 multiply_reduce_fusion.2
  160.9 0.2 mul.108
  161.1 2.5 copy.25
  163.6 1.2 copy.24
  164.8 0.4 fusion.11
  165.2 1.2 copy-done
  166.4 2.7 multiply_reduce_fusion
  169.1 1.3 convert_element_type.82
  170.4 0.5 convert_element_type.80
  170.9 2.0 fusion.47
  172.9 1.3 copy.20
  174.2 2.0 fusion.8
  176.2 1.8 reshape.57
  177.9 0.4 multiply_reduce_fusion.1
  178.3 0.7 stack.7
  179.0 1.6 pad_maximum_fusion
  180.7 32.6 %all-to-all-start.1 = ((f32[64,10,512]{2,1,0:T(8,128)}), f32[64,10,512]{2,1,0:T(8,128)S(1)}, u32[]{:S(2)}, u32[]{:S(2)}) async-start(f32[64,10,512]{2,1,0:T(8,128)} %pad_maximum_fusion), calls=%async_computation.1 | async-start | bytes 4194304 | tf_op jit(solution)/shard_map/all_to_all | solution.py:84
  213.3 150.9 %psum.7 = f32[]{:T(128)} all-reduce(f32[]{:T(128)} %get-tuple-element.4), channel_id=1, replica_groups=mesh['rows'=64,'cols'=8] {'rows','cols'}, use_global_device_ids=true, to_apply=%region_4.5 | all-reduce | flops 1 | bytes 8 | tf_op jit(solution)/shard_map/psum | solution.py:79
  365.1 0.6 fusion.26
  365.6 0.6 div.36
  (23 shorter events, 0.9 us)
Async XLA Ops:
  1.3 3.2 copy-start.4
  7.2 11.7 %copy-start.2 = (s32[1024]{0:T(1024)S(1)}, s32[1024]{0:T(1024)}, u32[]{:S(2)}) copy-start(s32[1024]{0:T(1024)} %param.5) | copy-start | bytes 12292
  7.2 11.8 %copy-start.3 = (f32[1024]{0:T(1024)S(1)}, f32[1024]{0:T(1024)}, u32[]{:S(2)}) copy-start(f32[1024]{0:T(1024)} %param.6) | copy-start | bytes 12292
  7.2 156.3 %all-to-all-start = ((f32[64,16,512]{2,1,0:T(8,128)}), f32[64,16,512]{2,1,0:T(8,128)S(1)}, u32[]{:S(2)}, u32[]{:S(2)}) async-start(f32[64,16,512]{2,1,0:T(8,128)} %bitcast.23), calls=%async_computation | async-start | bytes 4194304 | tf_op jit(solution)/shard_map/all_to_all | solution.py:56
  155.9 3.5 copy-start.1
  164.8 1.6 copy-start
  180.7 184.2 %all-to-all-start.1 = ((f32[64,10,512]{2,1,0:T(8,128)}), f32[64,10,512]{2,1,0:T(8,128)S(1)}, u32[]{:S(2)}, u32[]{:S(2)}) async-start(f32[64,10,512]{2,1,0:T(8,128)} %pad_maximum_fusion), calls=%async_computation.1 | async-start | bytes 4194304 | tf_op jit(solution)/shard_map/all_to_all | solution.py:84
where the time goes:
time: 367 us; the launch traced here: 366 us
  blocking collectives  287 us (78%)
  starting transfers between devices  44.3 us (12%)
  matrix products  15.4 us (4%)
  local copies, waits for them, and re-layouts  14.7 us (4%)
    psum x1, blocking collectives, local(): trace_sum = lax.psum(trace_part, ('rows', 'cols'))  151 us
    all_gather x1, blocking collectives, local(): whole = lax.all_gather(response * flips, 'rows', axis=0, tiled=True)  136 us
    all_to_all x1, starting transfers between devices, local(): lax.all_to_all(parts, 'rows', split_axis=0, concat_axis=0, tiled=True)  32.6 us
    all_to_all x1, starting transfers between devices, local(): lax.all_to_all(mixed.reshape(groups, share, width), 'rows', split_axis=0,...  11.7 us
    dot_general x11, matrix products, dot(): return jnp.dot(left, right, preferred_element_type=jnp.float32)  11.4 us
  transfers between devices with their start and end apart: 2, of which 0 were waited for; matrix products, arithmetic and copies ran while one was open for 2% of the time, Pallas kernels for 0%

commit v1 on v0

--- a/solution.py
+++ b/solution.py
@@ -44,7 +44,9 @@
     position = lax.axis_index("rows")
     share = height // groups
     flips = signs.astype(jnp.float32)
-    whole = lax.all_gather(response * flips, "rows", axis=0, tiled=True)
+    whole = jnp.concatenate(
+        lax.all_to_all(jnp.stack([response * flips] * lax.axis_size("rows")), "rows", 0, 0), 0
+    )
     side = 256
     square = whole.reshape(side, side)
     h_side = sylvester(side, jnp.bfloat16)

time: 367 us -> 252 us (0.69)
  blocking collectives: 287 us -> 144 us
  waiting for transfers between devices: 0.01 us -> 40.3 us
  starting transfers between devices: 44.3 us -> 29.8 us
    all_gather x1 -> x0, blocking collectives: 136 us -> none  [local(): whole = lax.all_gather(response * flips, 'rows', axis=0, tiled=True)]
    all_to_all x1, waiting for transfers between devices: 0.01 us -> 37.8 us  [local(): lax.all_to_all(mixed.reshape(groups, share, width), 'rows', split_axis=0,...]
    all_to_all x1, starting transfers between devices: 32.6 us -> 9.66 us  [local(): lax.all_to_all(parts, 'rows', split_axis=0, concat_axis=0, tiled=True)]
    all_to_all x0 -> x1, starting transfers between devices: none -> 11.6 us  [local(): lax.all_to_all(jnp.stack([response * flips] * lax.axis_size('rows')), 'ro...]
    psum x1, blocking collectives: 151 us -> 144 us  [local(): trace_sum = lax.psum(trace_part, ('rows', 'cols'))]
  transfers between devices with their start and end apart: 2 -> 3, of which waited for: 0 -> 2; matrix products, arithmetic and copies ran while one was open for 2% -> 6% of each run, Pallas kernels for 0% -> 0%
where the time goes in v1:
time: 252 us; the launch traced here: 251 us
  blocking collectives  144 us (57%)
  waiting for transfers between devices  40.3 us (16%)
  starting transfers between devices  29.8 us (12%)
  local copies, waits for them, and re-layouts  15.5 us (6%)
  matrix products  15.4 us (6%)
  other arithmetic  4.8 us (2%)
    psum x1, blocking collectives, local(): trace_sum = lax.psum(trace_part, ('rows', 'cols'))  144 us
    all_to_all x1, waiting for transfers between devices, local(): lax.all_to_all(mixed.reshape(groups, share, width), 'rows', split_axis=0,...  37.8 us
    all_to_all x1, starting transfers between devices, local(): lax.all_to_all(jnp.stack([response * flips] * lax.axis_size('rows')), 'ro...  11.6 us
    dot_general x11, matrix products, dot(): return jnp.dot(left, right, preferred_element_type=jnp.float32)  11.5 us
    all_to_all x1, starting transfers between devices, local(): lax.all_to_all(parts, 'rows', split_axis=0, concat_axis=0, tiled=True)  9.66 us
    all_to_all x1, starting transfers between devices, local(): lax.all_to_all(mixed.reshape(groups, share, width), 'rows', split_axis=0,...  8.53 us
  transfers between devices with their start and end apart: 3, of which 2 were waited for; matrix products, arithmetic and copies ran while one was open for 6% of the time, Pallas kernels for 0%

profile of v1, /device:TPU:27, one launch (start us, length us, event | category | flops | bytes accessed | tf_op | source)
XLA Modules:
  0.0 250.9 jit_solution(13751477860775774677)
XLA Ops:
  0.6 0.7 convert_multiply_fusion
  1.3 0.9 stack.6
  2.2 11.6 %all-to-all-start.1 = ((f32[64,1,1024]{2,1,0:T(1,128)}), f32[64,1,1024]{2,1,0:T(1,128)S(1)}, u32[]{:S(2)}, u32[]{:S(2)}) async-start(f32[64,1,1024]{2,1,0:T(1,128)} %stack.6), calls=%async_computation.1 | async-start | bytes 524288 | tf_op jit(solution)/shard_map/all_to_all | solution.py:48
  13.8 0.7 convert_element_type.74
  14.5 3.2 %fusion.3 = f32[1024,512]{1,0:T(8,128)S(1)} fusion(f32[1024,512]{1,0:T(8,128)} %param.4, f32[1024]{0:T(1024)S(1)} %convert_element_type.74), kind=kOutput, calls=%fused_computation.15 | convolution fusion | flops 1082130432 | bytes 4198400 | tf_op jit(solution)/shard_map/dot_general | solution.py:33
  17.7 2.7 %fusion.6 = f32[1024,512]{1,0:T(8,128)} fusion(f32[1024,512]{1,0:T(8,128)S(1)} %fusion.3, f32[1024,512]{1,0:T(8,128)S(1)} %copy-done.2, f32[1024]{0:T(1024)S(1)} %convert_element_type.74), kind=kOutput, calls=%fused_computation.18 | convolution fusion | flops 1082130432 | bytes 6295552 | tf_op jit(solution)/shard_map/dot_general | solution.py:33
  20.4 2.6 %all-to-all-done.1 = f32[64,1,1024]{2,1,0:T(1,128)S(1)} async-done(((f32[64,1,1024]{2,1,0:T(1,128)}), f32[64,1,1024]{2,1,0:T(1,128)S(1)}, u32[]{:S(2)}, u32[]{:S(2)}) %all-to-all-start.1) | async-done | bytes 262176 | tf_op jit(solution)/shard_map/all_to_all | solution.py:48
  23.0 8.5 %all-to-all-start = ((f32[64,16,512]{2,1,0:T(8,128)}), f32[64,16,512]{2,1,0:T(8,128)S(1)}, u32[]{:S(2)}, u32[]{:S(2)}) async-start(f32[64,16,512]{2,1,0:T(8,128)} %bitcast.23), calls=%async_computation | async-start | bytes 4194304 | tf_op jit(solution)/shard_map/all_to_all | solution.py:58
  31.6 0.6 reduce.1
  33.4 0.2 convolution_add_fusion.2
  33.6 2.0 reshape.63
  35.6 1.0 constant_dynamic-slice_fusion
  36.6 1.1 multiply_reduce_fusion.2
  38.2 2.5 copy.20
  40.7 37.8 %all-to-all-done = f32[64,16,512]{2,1,0:T(8,128)S(1)} async-done(((f32[64,16,512]{2,1,0:T(8,128)}), f32[64,16,512]{2,1,0:T(8,128)S(1)}, u32[]{:S(2)}, u32[]{:S(2)}) %all-to-all-start) | async-done | bytes 2097184 | tf_op jit(solution)/shard_map/all_to_all | solution.py:58
  78.5 1.2 copy.19
  79.7 0.4 fusion.11
  80.1 1.2 copy-done
  81.3 2.7 %multiply_reduce_fusion = (f32[]{:T(128)}, bf16[64,8192]{1,0:T(8,128)(2,1)S(1)}, bf16[64,8192]{1,0:T(8,128)(2,1)S(1)}, f32[64,8192]{1,0:T(8,128)}) fusion(f32[64,8192]{1,0:T(8,128)S(1)} %bitcast.22, f32[64,8192]{1,0:T(8,128)S(1)} %fusion.11, f32[64,8192]{1,0:T(8,128)S(1)} %bitcast.19), kind=kOutput, calls=%fused_computation.12 | convolution fusion | flops 72900608 | bytes 10485764 | tf_op jit(solution)/shard_map/dot_general | solution.py:33
  84.0 1.3 convert_element_type.82
  85.3 0.5 convert_element_type.80
  85.8 2.0 fusion.47
  87.8 1.3 copy.15
  89.1 2.0 fusion.8
  91.1 1.8 reshape.62
  92.9 0.4 multiply_reduce_fusion.1
  93.2 0.7 stack.8
  94.0 1.6 pad_maximum_fusion
  95.6 9.7 %all-to-all-start.2 = ((f32[64,10,512]{2,1,0:T(8,128)}), f32[64,10,512]{2,1,0:T(8,128)S(1)}, u32[]{:S(2)}, u32[]{:S(2)}) async-start(f32[64,10,512]{2,1,0:T(8,128)} %pad_maximum_fusion), calls=%async_computation.2 | async-start | bytes 4194304 | tf_op jit(solution)/shard_map/all_to_all | solution.py:86
  105.3 143.6 %psum.7 = f32[]{:T(128)} all-reduce(f32[]{:T(128)} %get-tuple-element.4), channel_id=1, replica_groups=mesh['rows'=64,'cols'=8] {'rows','cols'}, use_global_device_ids=true, to_apply=%region_4.5 | all-reduce | flops 1 | bytes 8 | tf_op jit(solution)/shard_map/psum | solution.py:81
  249.7 0.6 fusion.26
  250.3 0.6 div.36
  (22 shorter events, 2.0 us)
Async XLA Ops:
  2.2 20.8 %all-to-all-start.1 = ((f32[64,1,1024]{2,1,0:T(1,128)}), f32[64,1,1024]{2,1,0:T(1,128)S(1)}, u32[]{:S(2)}, u32[]{:S(2)}) async-start(f32[64,1,1024]{2,1,0:T(1,128)} %stack.6), calls=%async_computation.1 | async-start | bytes 524288 | tf_op jit(solution)/shard_map/all_to_all | solution.py:48
  14.5 3.2 %copy-start.2 = (f32[1024,512]{1,0:T(8,128)S(1)}, f32[1024,512]{1,0:T(8,128)}, u32[]{:S(2)}) copy-start(f32[1024,512]{1,0:T(8,128)} %param.4) | copy-start | bytes 6291460
  23.0 8.5 %copy-start.1 = (s32[8192]{0:T(1024)S(1)}, s32[8192]{0:T(1024)}, u32[]{:S(2)}) copy-start(s32[8192]{0:T(1024)} %param.7) | copy-start | bytes 98308
  23.0 55.5 %all-to-all-start = ((f32[64,16,512]{2,1,0:T(8,128)}), f32[64,16,512]{2,1,0:T(8,128)S(1)}, u32[]{:S(2)}, u32[]{:S(2)}) async-start(f32[64,16,512]{2,1,0:T(8,128)} %bitcast.23), calls=%async_computation | async-start | bytes 4194304 | tf_op jit(solution)/shard_map/all_to_all | solution.py:58
  79.7 1.6 copy-start
  95.6 153.9 %all-to-all-start.2 = ((f32[64,10,512]{2,1,0:T(8,128)}), f32[64,10,512]{2,1,0:T(8,128)S(1)}, u32[]{:S(2)}, u32[]{:S(2)}) async-start(f32[64,10,512]{2,1,0:T(8,128)} %pad_maximum_fusion), calls=%async_computation.2 | async-start | bytes 4194304 | tf_op jit(solution)/shard_map/all_to_all | solution.py:86
